TPU v7x, 32 devices: a whole 2x2x4 slice. The times are simulated.
32 devices in a mesh: row: 8 (over z, core), col: 4 (over y, x).
Axes of the slice: x: 2, y: 2, z: 4, core: 2. Of those that a mesh axis runs over, the one named last changes fastest.
Arguments:
- hidden: bfloat16 [1024, 2560], P('row'), may hold values from -4 to 4
- rel_bins: int32 [1024, 1024], P('row', 'col'), may hold values from 0 to 64, as said below
- attn_gain: float32 [2560], replicated, may hold values from 0.25 to 1.75
- w_query: bfloat16 [2560, 2560], P(None, 'col'), may hold values from -0.25 to 0.25
- w_key: bfloat16 [2560, 2560], P(None, 'col'), may hold values from -0.25 to 0.25
- w_value: bfloat16 [2560, 2560], P(None, 'col'), may hold values from -0.125 to 0.125
- w_out: bfloat16 [2560, 2560], P('col'), may hold values from -0.125 to 0.125
- final_gain: float32 [2560], P('col'), may hold values from 0.25 to 1.75
- w_single: bfloat16 [2560, 1024], P('col'), may hold values from -0.125 to 0.125
- w_second: bfloat16 [1024, 1024], replicated, may hold values from -0.1875 to 0.1875
- w_left: bfloat16 [1024, 128], replicated, may hold values from -0.1875 to 0.1875
- w_right: bfloat16 [1024, 128], replicated, may hold values from -0.1875 to 0.1875
- rel_table: bfloat16 [65, 128], replicated, may hold values from -6 to 6
- pair_gain: float32 [128], replicated, may hold values from 0.25 to 1.75
- w_expand: bfloat16 [128, 512], replicated, may hold values from -0.5 to 0.5
- w_contract: bfloat16 [512, 128], replicated, may hold values from -0.25 to 0.25
Outputs:
- pair_rep: bfloat16 [1024, 1024, 128], P('row', 'col')
Inputs may be any that keep to these rules, and one draw needn't show every extreme that they name: rel_bins[i, j] is the difference of the residue numbers of j and i, clipped to plus or minus (64) // 2 and shifted by (64) // 2.
All inputs are finite; a program needn't handle non-finite values.
Results may differ from a plain program's by a relative error of at most 0.013.
Values may be sent and summed in bfloat16 or wider, within the bound.
A program may use at most 128 MiB of HBM per device.

v0:
```python
import functools
import math

import jax
import jax.numpy as jnp
from jax import lax
from jax.experimental import pallas as pl
from jax.experimental.pallas import tpu as pltpu
from jax.sharding import PartitionSpec as P

HD = 64
MESH = pl.DeviceIdType.MESH


epsilon = 1e-05


def pair_kernel(bins_ref, left_ref, right_ref, table_ref, gain_ref, expand_ref, contract_ref, out_ref, table):
    block_rows, col_count = bins_ref.shape
    channels = right_ref.shape[1]
    right = right_ref[...].astype(jnp.float32)
    bins = table_ref.shape[0]

    @pl.when(pl.program_id(0) == 0)
    def _():
        table[...] = jnp.zeros_like(table)
        table[:bins] = table_ref[...]

    codes = lax.broadcasted_iota(jnp.int32, (table.shape[0], col_count), 0)
    hot = jnp.concatenate(
        [
            jnp.where(bins_ref[i : i + 1, :] == codes, 1.0, 0.0).astype(jnp.bfloat16)
            for i in range(block_rows)
        ],
        1,
    )
    part = lax.dot_general(
        hot, table[...], (((0,), (0,)), ((), ())), preferred_element_type=jnp.float32
    )
    pair_in = jnp.concatenate(
        [
            part[i * col_count : (i + 1) * col_count]
            + (right + left_ref[i : i + 1, :].astype(jnp.float32))
            for i in range(block_rows)
        ],
        0,
    )
    average = jnp.sum(pair_in, -1, keepdims=True) / channels
    variance = jnp.sum(pair_in * pair_in, -1, keepdims=True) / channels - average * average
    normed = ((pair_in - average) * lax.rsqrt(variance + epsilon) * gain_ref[...]).astype(
        jnp.bfloat16
    )
    expanded = jnp.dot(normed, expand_ref[...], preferred_element_type=jnp.float32)
    expanded = jnp.maximum(expanded.astype(jnp.bfloat16), 0)
    update = jnp.dot(expanded, contract_ref[...], preferred_element_type=jnp.float32)
    out_ref[...] = (pair_in + update).astype(out_ref.dtype).reshape(out_ref.shape)


def pair_stage(rel_bins, left, right, rel_table, pair_gain, w_expand, w_contract):
    row_count, col_count = rel_bins.shape
    channels = right.shape[1]
    block_rows = math.gcd(row_count, 32)
    bins_padded = -(-rel_table.shape[0] // 128) * 128
    whole = lambda array: pl.BlockSpec(array.shape, lambda i: (0, 0))
    gain = pair_gain.reshape(1, channels)
    return pl.pallas_call(
        pair_kernel,
        grid=(row_count // block_rows,),
        in_specs=[
            pl.BlockSpec((block_rows, col_count), lambda i: (i, 0)),
            pl.BlockSpec((block_rows, channels), lambda i: (i, 0)),
            whole(right),
            whole(rel_table),
            whole(gain),
            whole(w_expand),
            whole(w_contract),
        ],
        out_specs=pl.BlockSpec((block_rows, col_count, channels), lambda i: (i, 0, 0)),
        out_shape=jax.ShapeDtypeStruct((row_count, col_count, channels), jnp.bfloat16),
        scratch_shapes=[pltpu.VMEM((bins_padded, channels), jnp.bfloat16)],
        compiler_params=pltpu.CompilerParams(
            dimension_semantics=("arbitrary",), vmem_limit_bytes=56 << 20
        ),
    )(rel_bins, left, right, rel_table, gain, w_expand, w_contract)


def front_kernel(
    rows,
    cols,
    model_width,
    hidden_ref,
    own_hbm,
    attn_gain_ref,
    cos_ref,
    sin_ref,
    final_gain_ref,
    w_query_hbm,
    w_key_hbm,
    w_value_hbm,
    w_out_hbm,
    w_single_hbm,
    w_second_hbm,
    w_left_ref,
    w_right_ref,
    left_ref,
    right_ref,
    w_query,
    w_key,
    w_value,
    w_out,
    w_single,
    w_second,
    own,
    kv,
    query,
    totals,
    numerator,
    context,
    out_send,
    out_recv,
    stat_send,
    stat_recv,
    single_own,
    single_send,
    single_recv,
    sides,
    right_own,
    right_all,
    weight_sem,
    kv_send_sem,
    kv_recv_sem,
    out_send_sem,
    out_recv_sem,
    stat_send_sem,
    stat_recv_sem,
    single_send_sem,
    single_recv_sem,
    sides_send_sem,
    sides_recv_sem,
    right_send_sem,
    right_recv_sem,
):
    row = lax.axis_index("row")
    col = lax.axis_index("col")
    count = hidden_ref.shape[0]
    pairs = query.shape[0]
    features = w_single.shape[0]
    piece = single_own.shape[1]
    owners = rows // cols
    chips = rows // 2
    chip = row // 2
    core = row % 2
    partner = row + 1 - 2 * core

    own_columns = pl.ds(pl.multiple_of(col * features, 128), features)
    loads = []
    for index, (source, target) in enumerate(
        (
            (w_key_hbm, w_key),
            (w_value_hbm, w_value),
            (w_query_hbm, w_query),
            (w_out_hbm, w_out),
            (w_single_hbm, w_single),
            (w_second_hbm, w_second),
            (own_hbm.at[:, own_columns], own),
        )
    ):
        load = pltpu.make_async_copy(source, target, weight_sem.at[index])
        load.start()
        loads.append(load)

    barrier = pltpu.get_barrier_semaphore()
    is_owner = row // owners == col

    def greet(target_row, target_col):
        pl.semaphore_signal(
            barrier, inc=1, device_id=(target_row, target_col), device_id_type=MESH
        )

    greet(partner, col)

    @pl.when(chip + 1 < chips)
    def _():
        greet(row + 2, col)

    @pl.when(chip >= 1)
    def _():
        greet(row - 2, col)

    for slot in range(owners):
        for index in range(cols):

            @pl.when(jnp.logical_or(row != col * owners + slot, col != index))
            def _():
                greet(col * owners + slot, index)

    greetings = cols + rows
    greetings += jnp.where(chip + 1 < chips, 1, 0) + jnp.where(chip >= 1, 1, 0)
    greetings -= jnp.where(is_owner, 1, 0)
    for step in range(1, cols):
        pl.semaphore_signal(
            barrier, inc=1, device_id=(row, (col + step) % cols), device_id_type=MESH
        )

    stream = hidden_ref[...].astype(jnp.float32)
    average = jnp.sum(stream, -1, keepdims=True) / model_width
    variance = jnp.sum(stream * stream, -1, keepdims=True) / model_width - average * average
    attn_in = (
        (stream - average) * lax.rsqrt(variance + epsilon) * attn_gain_ref[...].reshape(1, -1)
    ).astype(jnp.bfloat16)
    cosine = cos_ref[...]
    sine = sin_ref[...]
    lane = lax.broadcasted_iota(jnp.int32, (count, 128), 1)
    first_half = lane % HD < HD // 2
    first_head = lane < HD

    def rope(vectors):
        turned = jnp.where(
            first_half,
            pltpu.roll(vectors, 128 - HD // 2, 1),
            pltpu.roll(vectors, HD // 2, 1),
        )
        return vectors * cosine + turned * sine

    def kv_copy(source, chunk, way, target):
        return pltpu.make_async_remote_copy(
            src_ref=kv.at[source, chunk],
            dst_ref=kv.at[source, chunk],
            send_sem=kv_send_sem.at[way, source, chunk],
            recv_sem=kv_recv_sem.at[source, chunk],
            device_id=(target, col),
            device_id_type=MESH,
        )

    def pass_on(source, chunk, right, left, act):
        if right:

            @pl.when(chip + 1 < chips)
            def _():
                act(kv_copy(source, chunk, 0, row + 2))

        if left:

            @pl.when(chip >= 1)
            def _():
                act(kv_copy(source, chunk, 1, row - 2))

        act(kv_copy(source, chunk, 2, partner))

    def start(copy):
        copy.start()

    def finish(copy):
        copy.wait_send()

    loads[0].wait()
    projected = jnp.dot(attn_in, w_key[...], preferred_element_type=jnp.float32)
    for pair in range(pairs):
        kv[row, 0, pair] = rope(projected[:, pair * 128 : pair * 128 + 128]).astype(jnp.bfloat16)
    pl.semaphore_wait(barrier, greetings)
    pass_on(row, 0, True, True, start)
    loads[1].wait()
    projected = jnp.dot(attn_in, w_value[...], preferred_element_type=jnp.float32)
    for pair in range(pairs):
        kv[row, 1, pair] = projected[:, pair * 128 : pair * 128 + 128].astype(jnp.bfloat16)
    pass_on(row, 1, True, True, start)
    loads[2].wait()
    projected = jnp.dot(attn_in, w_query[...], preferred_element_type=jnp.float32) * HD ** (-0.5)
    for pair in range(pairs):
        turned = rope(projected[:, pair * 128 : pair * 128 + 128])
        query[pair, :count] = jnp.where(first_head, turned, 0.0).astype(jnp.bfloat16)
        query[pair, count:] = jnp.where(first_head, 0.0, turned).astype(jnp.bfloat16)
    totals[...] = jnp.zeros_like(totals)
    numerator[...] = jnp.zeros_like(numerator)

    def attend(source):
        for pair in range(pairs):
            scores = lax.dot_general(
                query[pair],
                kv[source, 0, pair],
                (((1,), (1,)), ((), ())),
                preferred_element_type=jnp.float32,
            )
            weights = jnp.exp(scores)
            totals[pair] += weights
            numerator[pair] += jnp.dot(
                weights.astype(jnp.bfloat16),
                kv[source, 1, pair],
                preferred_element_type=jnp.float32,
            )

    def arrive(source):
        for chunk in range(2):
            kv_copy(source, chunk, 2, partner).wait_recv()

    attend(row)
    arrive(partner)
    attend(partner)

    @pl.loop(1, chips)
    def _(step):
        from_left = chip - step >= 0
        from_right = chip + step < chips
        for chunk in range(2):

            @pl.when(from_left)
            def _():
                source = row - 2 * step
                kv_copy(source, chunk, 2, partner).wait_recv()
                pass_on(source, chunk, True, False, start)

            @pl.when(from_right)
            def _():
                source = row + 2 * step
                kv_copy(source, chunk, 2, partner).wait_recv()
                pass_on(source, chunk, False, True, start)

        @pl.when(from_left)
        def _():
            attend(row - 2 * step)
            arrive(partner - 2 * step)
            attend(partner - 2 * step)

        @pl.when(from_right)
        def _():
            attend(row + 2 * step)
            arrive(partner + 2 * step)
            attend(partner + 2 * step)

    for pair in range(pairs):
        shares = numerator[pair] / jnp.sum(totals[pair], -1, keepdims=True)
        context[:, pair * 128 : pair * 128 + 128] = jnp.where(
            first_head, shares[:count], shares[count:]
        ).astype(jnp.bfloat16)

    def out_copy(source, target):
        return pltpu.make_async_remote_copy(
            src_ref=out_send.at[target],
            dst_ref=out_recv.at[source],
            send_sem=out_send_sem.at[target],
            recv_sem=out_recv_sem.at[source],
            device_id=(row, target),
            device_id_type=MESH,
        )

    def out_part(target):
        columns = pl.ds(pl.multiple_of(target * features, 128), features)
        return jnp.dot(context[...], w_out[:, columns], preferred_element_type=jnp.float32)

    others = [(col + step) % cols for step in range(1, cols)]
    loads[3].wait()
    for target in others:
        out_send[target] = out_part(target).astype(jnp.bfloat16)
        out_copy(col, target).start()
    loads[6].wait()
    resid = own[...].astype(jnp.float32) + out_part(col)
    for source in others:
        out_copy(source, source).wait_recv()
        resid += out_recv[source].astype(jnp.float32)

    def stat_copy(source, target):
        return pltpu.make_async_remote_copy(
            src_ref=stat_send,
            dst_ref=stat_recv.at[source],
            send_sem=stat_send_sem.at[target],
            recv_sem=stat_recv_sem.at[source],
            device_id=(row, target),
            device_id_type=MESH,
        )

    sum_first = jnp.sum(resid, -1, keepdims=True)
    sum_second = jnp.sum(resid * resid, -1, keepdims=True)
    sums = jnp.transpose(jnp.where(lane < 4, sum_first, sum_second))[:8]
    stat_send[...] = sums
    for target in others:
        stat_copy(col, target).start()
    for source in others:
        stat_copy(source, source).wait_recv()
        sums += stat_recv[source]
    sums = jnp.transpose(jnp.concatenate([sums] * 16, 0))
    average = sums[:, 0:1] / model_width
    variance = sums[:, 4:5] / model_width - average * average
    final = (
        (resid - average) * lax.rsqrt(variance + epsilon) * final_gain_ref[...].reshape(1, -1)
    ).astype(jnp.bfloat16)

    def single_copy(source, target):
        return pltpu.make_async_remote_copy(
            src_ref=single_send.at[target],
            dst_ref=single_recv.at[source],
            send_sem=single_send_sem.at[target],
            recv_sem=single_recv_sem.at[source],
            device_id=(row, target),
            device_id_type=MESH,
        )

    loads[4].wait()
    part = jnp.dot(final, w_single[...], preferred_element_type=jnp.float32)
    for index in range(cols):
        block = part[index * piece : (index + 1) * piece]
        single_own[index] = block
        single_send[index] = block.astype(jnp.bfloat16)
    for target in others:
        single_copy(col, target).start()
    summed = single_own[col]
    for source in others:
        single_copy(source, source).wait_recv()
        summed += single_recv[source].astype(jnp.float32)
    lifted = jnp.maximum(summed, 0.0).astype(jnp.bfloat16)
    loads[5].wait()
    single = jnp.dot(lifted, w_second[...], preferred_element_type=jnp.float32)
    single = single.astype(jnp.bfloat16)

    def sides_copy(source, target):
        return pltpu.make_async_remote_copy(
            src_ref=sides.at[source],
            dst_ref=sides.at[source],
            send_sem=sides_send_sem.at[target],
            recv_sem=sides_recv_sem.at[source],
            device_id=(row, target),
            device_id_type=MESH,
        )

    def right_copy(slot, index, step):
        return pltpu.make_async_remote_copy(
            src_ref=right_own,
            dst_ref=right_all.at[slot, index],
            send_sem=right_send_sem.at[step],
            recv_sem=right_recv_sem.at[slot, index],
            device_id=((row + step) % rows, row // owners),
            device_id_type=MESH,
        )

    right_own[...] = jnp.dot(
        single, w_right_ref[...], preferred_element_type=jnp.float32
    ).astype(jnp.bfloat16)
    for step in range(1, rows):
        right_copy(row % owners, col, step).start()

    @pl.when(jnp.logical_not(is_owner))
    def _():
        right_copy(row % owners, col, 0).start()

    sides[col] = jnp.dot(single, w_left_ref[...], preferred_element_type=jnp.float32).astype(
        jnp.bfloat16
    )
    for target in others:
        sides_copy(col, target).start()

    @pl.when(is_owner)
    def _():
        right_all[row % owners, col] = right_own[...]

    for source in others:
        sides_copy(source, source).wait_recv()
    for index in range(cols):
        left_ref[index * piece : (index + 1) * piece] = sides[index]
    for slot in range(owners):
        for index in range(cols):

            @pl.when(jnp.logical_or(row != col * owners + slot, col != index))
            def _():
                right_copy(slot, index, 1).wait_recv()

            start_row = slot * count + index * piece
            right_ref[start_row : start_row + piece] = right_all[slot, index]

    for chunk in range(2):
        pass_on(row, chunk, True, True, finish)

    @pl.loop(1, chips)
    def _(step):
        for chunk in range(2):

            @pl.when(chip - step >= 0)
            def _():
                pass_on(row - 2 * step, chunk, True, False, finish)

            @pl.when(chip + step < chips)
            def _():
                pass_on(row + 2 * step, chunk, False, True, finish)

    for target in others:
        out_copy(col, target).wait_send()
        stat_copy(col, target).wait_send()
        single_copy(col, target).wait_send()
        sides_copy(col, target).wait_send()

    for step in range(1, rows):
        right_copy(row % owners, col, step).wait_send()

    @pl.when(jnp.logical_not(is_owner))
    def _():
        right_copy(row % owners, col, 0).wait_send()


def padded(array, axis, size, groups=1):
    width = array.shape[axis] // groups
    if width == size:
        return array
    shape = array.shape
    array = array.reshape(shape[:axis] + (groups, width) + shape[axis + 1 :])
    pads = [(0, 0)] * array.ndim
    pads[axis + 1] = (0, size - width)
    array = jnp.pad(array, pads)
    return array.reshape(shape[:axis] + (groups * size,) + shape[axis + 1 :])


def local(
    hidden,
    rel_bins,
    attn_gain,
    w_query,
    w_key,
    w_value,
    w_out,
    final_gain,
    w_single,
    w_second,
    w_left,
    w_right,
    rel_table,
    pair_gain,
    w_expand,
    w_contract,
):
    rows = lax.axis_size("row")
    cols = lax.axis_size("col")
    count, model_width = hidden.shape
    width = -(-w_query.shape[1] // 128) * 128
    features = -(-w_single.shape[0] // 128) * 128
    pairs = width // 128
    piece = count // cols
    owners = rows // cols
    single_width = w_second.shape[0]
    channels = w_left.shape[1]
    positions = lax.axis_index("row") * count + jnp.arange(count, dtype=jnp.int32)
    frequency = jnp.exp(
        jnp.arange(HD // 2, dtype=jnp.float32) * (-2.0 * math.log(10000.0) / HD)
    )
    angles = positions.astype(jnp.float32)[:, None] * frequency[None, :]
    cosine = jnp.cos(angles)
    sine = jnp.sin(angles)
    cosine = jnp.concatenate([cosine] * 4, -1)
    sine = jnp.concatenate([-sine, sine, -sine, sine], -1)
    weights = (
        padded(w_query, 1, width),
        padded(w_key, 1, width),
        padded(w_value, 1, width),
        padded(padded(w_out, 0, width), 1, features, cols),
        padded(w_single, 0, features),
        w_second,
    )
    vmem = pl.BlockSpec(memory_space=pltpu.VMEM)
    anywhere = pl.BlockSpec(memory_space=pl.ANY)
    bf16 = jnp.bfloat16
    f32 = jnp.float32
    dma = pltpu.SemaphoreType.DMA
    left, right = pl.pallas_call(
        functools.partial(front_kernel, rows, cols, model_width),
        out_shape=(
            jax.ShapeDtypeStruct((count, channels), bf16),
            jax.ShapeDtypeStruct((owners * count, channels), bf16),
        ),
        in_specs=[vmem, anywhere] + [vmem] * 4 + [anywhere] * 6 + [vmem] * 2,
        out_specs=(vmem, vmem),
        scratch_shapes=[pltpu.VMEM(weight.shape, bf16) for weight in weights]
        + [
            pltpu.VMEM((count, features), bf16),
            pltpu.VMEM((rows, 2, pairs, count, 128), bf16),
            pltpu.VMEM((pairs, 2 * count, 128), bf16),
            pltpu.VMEM((pairs, 2 * count, count), f32),
            pltpu.VMEM((pairs, 2 * count, 128), f32),
            pltpu.VMEM((count, width), bf16),
            pltpu.VMEM((cols, count, features), bf16),
            pltpu.VMEM((cols, count, features), bf16),
            pltpu.VMEM((8, count), f32),
            pltpu.VMEM((cols, 8, count), f32),
            pltpu.VMEM((cols, piece, single_width), f32),
            pltpu.VMEM((cols, piece, single_width), bf16),
            pltpu.VMEM((cols, piece, single_width), bf16),
            pltpu.VMEM((cols, piece, channels), bf16),
            pltpu.VMEM((piece, channels), bf16),
            pltpu.VMEM((owners, cols, piece, channels), bf16),
            dma((7,)),
            dma((3, rows, 2)),
            dma((rows, 2)),
            dma((cols,)),
            dma((cols,)),
            dma((cols,)),
            dma((cols,)),
            dma((cols,)),
            dma((cols,)),
            dma((cols,)),
            dma((cols,)),
            dma((rows,)),
            dma((owners, cols)),
        ],
        compiler_params=pltpu.CompilerParams(
            collective_id=0, has_side_effects=True, vmem_limit_bytes=56 << 20
        ),
    )(
        hidden,
        padded(hidden, 1, features, cols),
        attn_gain,
        cosine,
        sine,
        padded(final_gain, 0, features),
        *weights,
        w_left,
        w_right,
    )
    return pair_stage(rel_bins, left, right, rel_table, pair_gain, w_expand, w_contract)


def solution(mesh):
    in_specs = (
        P("row", None),
        P("row", "col"),
        P(),
        P(None, "col"),
        P(None, "col"),
        P(None, "col"),
        P("col", None),
        P("col"),
        P("col", None),
        P(),
        P(),
        P(),
        P(),
        P(),
        P(),
        P(),
    )
    out_specs = P("row", "col", None)
    return jax.shard_map(local, mesh=mesh, in_specs=in_specs, out_specs=out_specs, check_vma=False)
```

profile of v0, /device:TPU:0, one launch (start us, length us, event | category | flops | bytes accessed | tf_op | source)
XLA Modules:
  0.0 80.5 jit_solution(2041163930758256081)
XLA Ops:
  0.0 0.3 fusion
  0.3 0.8 %pad_maximum_fusion = (f32[128,128]{1,0:T(8,128)}, f32[128,128]{1,0:T(8,128)}) fusion(f32[128,32]{1,0:T(8,128)S(1)} %get-tuple-element.11, f32[128,32]{1,0:T(8,128)S(1)} %get-tuple-element.10, f32[128,32]{1,0:T(8,128)S(1)} %get-tuple-element.9), kind=kLoop, calls=%fused_computation.2 | loop fusion | flops 98304 | bytes 180224 | tf_op jit(solution)/shard_map/concatenate | solution.py:544
  1.1 55.9 %shard_map.154 = (bf16[128,128]{1,0:T(8,128)(2,1)}, bf16[256,128]{1,0:T(8,128)(2,1)}) custom-call(bf16[128,2560]{1,0:T(8,128)(2,1)} %own_hbm.1, bf16[128,2560]{1,0:T(8,128)(2,1)} %own_hbm.1, f32[2560]{0:T(1024)} %attn_gain_ref.1, f32[128,128]{1,0:T(8,128)} %get-tuple-element.12.cos_ref, f32[128,128]{1,0:T(8,128)} %get-tuple-element.13.sin_ref, ...), custom_call_target="tpu_custom_call" | custom-call | tf_op jit(solution)/shard_map/pallas_call | solution.py:559
  57.0 23.4 %shard_map.155 = bf16[128,256,128]{2,1,0:T(8,128)(2,1)} custom-call(s32[128,256]{1,0:T(8,128)} %bins_ref.1, bf16[128,128]{1,0:T(8,128)(2,1)} %get-tuple-element.7.left_ref, bf16[256,128]{1,0:T(8,128)(2,1)} %get-tuple-element.8.right_ref, bf16[65,128]{1,0:T(8,128)(2,1)} %table_ref.1, f32[1,128]{1,0:T(1,128)} %bitcast.1, bf16[128,512]{1,0:T(8,128)(2,1)} %expand_ref.1, ...), custom_call_target="tpu_custom_call" | custom-call | tf_op jit(solution)/shard_map/pallas_call | solution.py:66
  (2 shorter events, 0.0 us)
where the time goes:
time: 80.6 us; the launch traced here: 80.5 us
  Pallas kernels  79.3 us (98%)
  other arithmetic  1.14 us (1%)
    pallas_call x1, Pallas kernels, local(): pl.pallas_call(functools.partial(front_kernel, rows, cols, model_width),...  55.9 us
    pallas_call x1, Pallas kernels, pair_stage(): pl.pallas_call(pair_kernel, grid=(row_count // block_rows,), in_specs=[pl...  23.4 us

commit v1 on v0

--- a/solution.py
+++ b/solution.py
@@ -3,6 +3,7 @@
 
 import jax
 import jax.numpy as jnp
+import numpy as np
 from jax import lax
 from jax.experimental import pallas as pl
 from jax.experimental.pallas import tpu as pltpu
@@ -494,6 +495,610 @@
         right_copy(row % owners, col, 0).wait_send()
 
 
+def plane_kernel(
+    rows,
+    cols,
+    model_width,
+    hidden_ref,
+    own_hbm,
+    attn_gain_ref,
+    cos_ref,
+    sin_ref,
+    cos_step_ref,
+    sin_step_ref,
+    final_gain_ref,
+    w_query_hbm,
+    w_key_hbm,
+    w_value_hbm,
+    w_out_hbm,
+    w_single_hbm,
+    w_second_hbm,
+    w_left_ref,
+    w_right_ref,
+    bins_ref,
+    table_ref,
+    left_ref,
+    right_ref,
+    rel_hbm,
+    w_query,
+    w_key,
+    w_value,
+    w_out,
+    w_single,
+    w_second,
+    own,
+    piece_send,
+    far,
+    kv,
+    query,
+    totals,
+    numerator,
+    context,
+    out_send,
+    out_recv,
+    stat_send,
+    stat_recv,
+    gain_sums,
+    single_own,
+    single_send,
+    single_recv,
+    sides,
+    right_own,
+    right_all,
+    table,
+    rel_slots,
+    weight_sem,
+    far_out_sem,
+    far_send_sem,
+    far_recv_sem,
+    kv_send_sem,
+    kv_recv_sem,
+    out_send_sem,
+    out_recv_sem,
+    stat_send_sem,
+    stat_recv_sem,
+    single_send_sem,
+    single_recv_sem,
+    sides_send_sem,
+    sides_recv_sem,
+    right_send_sem,
+    right_recv_sem,
+    gain_send_sem,
+    gain_recv_sem,
+    rel_sem,
+):
+    row = lax.axis_index("row")
+    col = lax.axis_index("col")
+    count = hidden_ref.shape[0]
+    pairs = query.shape[0]
+    features = w_single.shape[0]
+    piece = single_own.shape[1]
+    owners = rows // cols
+    chips = rows // 2
+    chip = row // 2
+    core = row % 2
+    partner = row + 1 - 2 * core
+    outer = jnp.logical_or(chip == 0, chip == chips - 1)
+    farthest = (chips - 1 - chip) * 2 + core
+    side = col + 1 - 2 * (col % 2)
+    across = (col + 2) % cols
+    corner = cols - 1 - col
+
+    own_columns = pl.ds(pl.multiple_of(col * features, 128), features)
+    loads = []
+    for index, (source, target) in enumerate(
+        (
+            (w_key_hbm, w_key),
+            (w_value_hbm, w_value),
+            (w_query_hbm, w_query),
+            (w_out_hbm, w_out),
+            (w_single_hbm, w_single),
+            (w_second_hbm, w_second),
+            (own_hbm.at[:, own_columns], own),
+        )
+    ):
+        load = pltpu.make_async_copy(source, target, weight_sem.at[index])
+        load.start()
+        loads.append(load)
+
+    barrier = pltpu.get_barrier_semaphore()
+    is_owner = row // owners == col
+
+    def greet(target_row, target_col):
+        pl.semaphore_signal(
+            barrier, inc=1, device_id=(target_row, target_col), device_id_type=MESH
+        )
+
+    greet(partner, col)
+
+    @pl.when(outer)
+    def _():
+        greet(farthest, col)
+
+    @pl.when(chip + 1 < chips)
+    def _():
+        greet(row + 2, col)
+
+    @pl.when(chip >= 1)
+    def _():
+        greet(row - 2, col)
+
+    for slot in range(owners):
+        for index in range(cols):
+
+            @pl.when(jnp.logical_or(row != col * owners + slot, col != index))
+            def _():
+                greet(col * owners + slot, index)
+
+    greetings = cols + rows + jnp.where(outer, 1, 0)
+    greetings += jnp.where(chip + 1 < chips, 1, 0) + jnp.where(chip >= 1, 1, 0)
+    greetings -= jnp.where(is_owner, 1, 0)
+    for step in range(1, cols):
+        pl.semaphore_signal(
+            barrier, inc=1, device_id=(row, (col + step) % cols), device_id_type=MESH
+        )
+
+    def normalize(values):
+        stream = values.astype(jnp.float32)
+        average = jnp.sum(stream, -1, keepdims=True) / model_width
+        variance = jnp.sum(stream * stream, -1, keepdims=True) / model_width - average * average
+        return (
+            (stream - average) * lax.rsqrt(variance + epsilon) * attn_gain_ref[...].reshape(1, -1)
+        ).astype(jnp.bfloat16)
+
+    half = piece // 2
+
+    @pl.when(outer)
+    def _():
+        for part in range(2):
+            first = pl.multiple_of(col * piece + part * half, half)
+            piece_send[part] = normalize(hidden_ref[pl.ds(first, half)])
+
+    lane = lax.broadcasted_iota(jnp.int32, (count, 128), 1)
+    first_half = lane % HD < HD // 2
+    first_head = lane < HD
+
+    def tables(source):
+        cosine = cos_ref[...]
+        sine = sin_ref[...]
+        cos_step = cos_step_ref[pl.ds(source, 1), :]
+        sin_step = sin_step_ref[pl.ds(source, 1), :]
+        turned = sine * cos_step + cosine * sin_step
+        return cosine * cos_step - sine * sin_step, jnp.where(first_half, -turned, turned)
+
+    def rope(vectors, cosine, sine):
+        turned = jnp.where(
+            first_half,
+            pltpu.roll(vectors, 128 - HD // 2, 1),
+            pltpu.roll(vectors, HD // 2, 1),
+        )
+        return vectors * cosine + turned * sine
+
+    def far_copy(owner, part, way, target):
+        return pltpu.make_async_remote_copy(
+            src_ref=far.at[owner, part],
+            dst_ref=far.at[owner, part],
+            send_sem=far_send_sem.at[way, part],
+            recv_sem=far_recv_sem.at[owner, part],
+            device_id=(row, target),
+            device_id_type=MESH,
+        )
+
+    def far_out(part):
+        return pltpu.make_async_remote_copy(
+            src_ref=piece_send.at[part],
+            dst_ref=far.at[col, part],
+            send_sem=far_out_sem.at[part],
+            recv_sem=far_recv_sem.at[col, part],
+            device_id=(farthest, col),
+            device_id_type=MESH,
+        )
+
+    def share(part, act):
+        act(far_copy(col, part, 0, side))
+        act(far_copy(col, part, 1, across))
+
+    def share_corner(part, act):
+        if part == 0:
+            act(far_copy(side, part, 2, across))
+        else:
+            act(far_copy(across, part, 2, side))
+
+    def far_wait(owner, part):
+        far_copy(owner, part, 0, side).wait_recv()
+
+    def kv_copy(source, chunk, way, target):
+        return pltpu.make_async_remote_copy(
+            src_ref=kv.at[source, chunk],
+            dst_ref=kv.at[source, chunk],
+            send_sem=kv_send_sem.at[way, source, chunk],
+            recv_sem=kv_recv_sem.at[source, chunk],
+            device_id=(target, col),
+            device_id_type=MESH,
+        )
+
+    def pass_on(source, chunk, right, left, act):
+        if right:
+
+            @pl.when(chip + 1 < chips)
+            def _():
+                act(kv_copy(source, chunk, 0, row + 2))
+
+        if left:
+
+            @pl.when(chip >= 1)
+            def _():
+                act(kv_copy(source, chunk, 1, row - 2))
+
+        act(kv_copy(source, chunk, 2, partner))
+
+    def start(copy):
+        copy.start()
+
+    def finish(copy):
+        copy.wait_send()
+
+    pl.semaphore_wait(barrier, greetings)
+
+    @pl.when(outer)
+    def _():
+        for part in range(2):
+            far_out(part).start()
+
+    def keys_of(rows_in, source):
+        cosine, sine = tables(source)
+        projected = jnp.dot(rows_in, w_key[...], preferred_element_type=jnp.float32)
+        for pair in range(pairs):
+            kv[source, 0, pair] = rope(
+                projected[:, pair * 128 : pair * 128 + 128], cosine, sine
+            ).astype(jnp.bfloat16)
+
+    def values_of(rows_in, source):
+        projected = jnp.dot(rows_in, w_value[...], preferred_element_type=jnp.float32)
+        for pair in range(pairs):
+            kv[source, 1, pair] = projected[:, pair * 128 : pair * 128 + 128].astype(jnp.bfloat16)
+
+    attn_in = normalize(hidden_ref[...])
+    loads[0].wait()
+    keys_of(attn_in, row)
+    pass_on(row, 0, True, True, start)
+    loads[1].wait()
+    values_of(attn_in, row)
+    pass_on(row, 1, True, True, start)
+
+    @pl.when(outer)
+    def _():
+        for part in range(2):
+            far_wait(col, part)
+            share(part, start)
+
+    def gain_copy(source, target):
+        return pltpu.make_async_remote_copy(
+            src_ref=gain_sums.at[source],
+            dst_ref=gain_sums.at[source],
+            send_sem=gain_send_sem.at[target],
+            recv_sem=gain_recv_sem.at[source],
+            device_id=(row, target),
+            device_id_type=MESH,
+        )
+
+    others = [(col + step) % cols for step in range(1, cols)]
+    loads[2].wait()
+    cosine, sine = tables(row)
+    projected = jnp.dot(attn_in, w_query[...], preferred_element_type=jnp.float32) * HD ** (-0.5)
+    for pair in range(pairs):
+        turned = rope(projected[:, pair * 128 : pair * 128 + 128], cosine, sine)
+        query[pair, :count] = jnp.where(first_head, turned, 0.0).astype(jnp.bfloat16)
+        query[pair, count:] = jnp.where(first_head, 0.0, turned).astype(jnp.bfloat16)
+    bins = table_ref.shape[0]
+    table[...] = jnp.zeros_like(table)
+    table[:bins] = table_ref[...]
+    slot_rows = rel_slots.shape[1]
+    col_count = bins_ref.shape[1]
+    slots = bins_ref.shape[0] // slot_rows
+
+    def rel_copy(index):
+        return pltpu.make_async_copy(
+            rel_slots.at[index % 2],
+            rel_hbm.at[pl.ds(pl.multiple_of(index * slot_rows, slot_rows), slot_rows)],
+            rel_sem.at[index % 2],
+        )
+
+    def spell(begin, end):
+        @pl.loop(begin, end)
+        def _(index):
+            @pl.when(index >= 2)
+            def _():
+                rel_copy(index - 2).wait()
+
+            picked = bins_ref[pl.ds(pl.multiple_of(index * slot_rows, slot_rows), slot_rows)]
+            codes = lax.broadcasted_iota(jnp.int32, (table.shape[0], col_count), 0)
+            hot = jnp.concatenate(
+                [
+                    jnp.where(picked[i : i + 1, :] == codes, 1.0, 0.0).astype(jnp.bfloat16)
+                    for i in range(slot_rows)
+                ],
+                1,
+            )
+            chosen = lax.dot_general(
+                hot, table[...], (((0,), (0,)), ((), ())), preferred_element_type=jnp.float32
+            )
+            rel_slots[index % 2] = chosen.astype(jnp.bfloat16).reshape(rel_slots.shape[1:])
+            rel_copy(index).start()
+
+    totals[...] = jnp.zeros_like(totals)
+    numerator[...] = jnp.zeros_like(numerator)
+
+    def attend(source):
+        for pair in range(pairs):
+            scores = lax.dot_general(
+                query[pair],
+                kv[source, 0, pair],
+                (((1,), (1,)), ((), ())),
+                preferred_element_type=jnp.float32,
+            )
+            weights = jnp.exp(scores)
+            totals[pair] += weights
+            numerator[pair] += jnp.dot(
+                weights.astype(jnp.bfloat16),
+                kv[source, 1, pair],
+                preferred_element_type=jnp.float32,
+            )
+
+    def arrive(source):
+        for chunk in range(2):
+            kv_copy(source, chunk, 2, partner).wait_recv()
+
+    attend(row)
+    loads[4].wait()
+    gain = final_gain_ref[...].reshape(1, -1)
+    coarse = gain.astype(jnp.bfloat16)
+    fine = (gain - coarse.astype(jnp.float32)).astype(jnp.bfloat16)
+    gains = jnp.concatenate([jnp.broadcast_to(part, (16, features)) for part in (coarse, fine)], 0)
+    gained = jnp.dot(gains, w_single[...], preferred_element_type=jnp.float32)
+    gain_sums[col] = gained[:8] + gained[16:24]
+    for target in others:
+        gain_copy(col, target).start()
+
+    @pl.when(outer)
+    def _():
+        far_wait(side, 0)
+        share_corner(0, start)
+        far_wait(across, 1)
+        share_corner(1, start)
+
+    arrive(partner)
+    attend(partner)
+    spell(0, slots // 2)
+
+    def near(step, onward):
+        from_left = chip - step >= 0
+        from_right = chip + step < chips
+        for chunk in range(2):
+
+            @pl.when(from_left)
+            def _():
+                source = row - 2 * step
+                kv_copy(source, chunk, 2, partner).wait_recv()
+                pass_on(source, chunk, onward, False, start)
+
+            @pl.when(from_right)
+            def _():
+                source = row + 2 * step
+                kv_copy(source, chunk, 2, partner).wait_recv()
+                pass_on(source, chunk, False, onward, start)
+
+        @pl.when(from_left)
+        def _():
+            attend(row - 2 * step)
+            arrive(partner - 2 * step)
+            attend(partner - 2 * step)
+
+        @pl.when(from_right)
+        def _():
+            attend(row + 2 * step)
+            arrive(partner + 2 * step)
+            attend(partner + 2 * step)
+
+    for step in range(1, chips - 1):
+        near(step, step < chips - 2)
+        if step == 1:
+            spell(slots // 2, slots)
+
+            @pl.when(outer)
+            def _():
+                far_wait(side, 1)
+                far_wait(across, 0)
+                for part in range(2):
+                    far_wait(corner, part)
+                rows_in = far[...].reshape(count, model_width)
+                keys_of(rows_in, farthest)
+                pass_on(farthest, 0, False, False, start)
+                values_of(rows_in, farthest)
+                pass_on(farthest, 1, False, False, start)
+                other = farthest + partner - row
+                attend(farthest)
+                arrive(other)
+                attend(other)
+
+    for pair in range(pairs):
+        shares = numerator[pair] / jnp.sum(totals[pair], -1, keepdims=True)
+        context[:, pair * 128 : pair * 128 + 128] = jnp.where(
+            first_head, shares[:count], shares[count:]
+        ).astype(jnp.bfloat16)
+
+    def out_copy(source, target):
+        return pltpu.make_async_remote_copy(
+            src_ref=out_send.at[target],
+            dst_ref=out_recv.at[source],
+            send_sem=out_send_sem.at[target],
+            recv_sem=out_recv_sem.at[source],
+            device_id=(row, target),
+            device_id_type=MESH,
+        )
+
+    def out_part(target):
+        columns = pl.ds(pl.multiple_of(target * features, 128), features)
+        return jnp.dot(context[...], w_out[:, columns], preferred_element_type=jnp.float32)
+
+    loads[3].wait()
+    for target in others:
+        out_send[target] = out_part(target).astype(jnp.bfloat16)
+        out_copy(col, target).start()
+    loads[6].wait()
+    resid = own[...].astype(jnp.float32) + out_part(col)
+    for source in others:
+        out_copy(source, source).wait_recv()
+        resid += out_recv[source].astype(jnp.float32)
+
+    def stat_copy(source, target):
+        return pltpu.make_async_remote_copy(
+            src_ref=stat_send.at[target],
+            dst_ref=stat_recv.at[source],
+            send_sem=stat_send_sem.at[target],
+            recv_sem=stat_recv_sem.at[source],
+            device_id=(row, target),
+            device_id_type=MESH,
+        )
+
+    middle = jnp.sum(resid, -1, keepdims=True) / features
+    centred = resid - middle
+    spread_sum = jnp.sum(centred * centred, -1, keepdims=True)
+    stats = jnp.where(lane < 1, middle, spread_sum)
+    for index in range(cols):
+        stat_send[index] = stats[index * piece : (index + 1) * piece]
+    for target in others:
+        stat_copy(col, target).start()
+    final = (centred * final_gain_ref[...].reshape(1, -1)).astype(jnp.bfloat16)
+
+    def single_copy(source, target):
+        return pltpu.make_async_remote_copy(
+            src_ref=single_send.at[target],
+            dst_ref=single_recv.at[source],
+            send_sem=single_send_sem.at[target],
+            recv_sem=single_recv_sem.at[source],
+            device_id=(row, target),
+            device_id_type=MESH,
+        )
+
+    part = jnp.dot(final, w_single[...], preferred_element_type=jnp.float32)
+    for index in range(cols):
+        block = part[index * piece : (index + 1) * piece]
+        single_own[index] = block
+        single_send[index] = block.astype(jnp.bfloat16)
+    for target in others:
+        single_copy(col, target).start()
+    for source in others:
+        stat_copy(source, source).wait_recv()
+        gain_copy(source, source).wait_recv()
+    stat_recv[col] = stat_send[col]
+    middles = [stat_recv[index][:, 0:1] for index in range(cols)]
+    average = sum(middles) / cols
+    variance = sum(stat_recv[index][:, 1:2] for index in range(cols)) / model_width
+    variance += sum((middles[index] - average) * (middles[index] - average) for index in range(cols)) / cols
+    scale = lax.rsqrt(variance + epsilon)
+    summed = single_own[col]
+    for index in range(cols):
+        summed += (middles[index] - average) * gain_sums[index][0:1]
+    for source in others:
+        single_copy(source, source).wait_recv()
+        summed += single_recv[source].astype(jnp.float32)
+    lifted = jnp.maximum(summed * scale, 0.0).astype(jnp.bfloat16)
+    loads[5].wait()
+    single = jnp.dot(lifted, w_second[...], preferred_element_type=jnp.float32)
+    single = single.astype(jnp.bfloat16)
+
+    def sides_copy(source, target):
+        return pltpu.make_async_remote_copy(
+            src_ref=sides.at[source],
+            dst_ref=sides.at[source],
+            send_sem=sides_send_sem.at[target],
+            recv_sem=sides_recv_sem.at[source],
+            device_id=(row, target),
+            device_id_type=MESH,
+        )
+
+    def right_copy(slot, index, step):
+        return pltpu.make_async_remote_copy(
+            src_ref=right_own,
+            dst_ref=right_all.at[slot, index],
+            send_sem=right_send_sem.at[step],
+            recv_sem=right_recv_sem.at[slot, index],
+            device_id=((row + step) % rows, row // owners),
+            device_id_type=MESH,
+        )
+
+    right_own[...] = jnp.dot(
+        single, w_right_ref[...], preferred_element_type=jnp.float32
+    ).astype(jnp.bfloat16)
+    for step in range(1, rows):
+        right_copy(row % owners, col, step).start()
+
+    @pl.when(jnp.logical_not(is_owner))
+    def _():
+        right_copy(row % owners, col, 0).start()
+
+    sides[col] = jnp.dot(single, w_left_ref[...], preferred_element_type=jnp.float32).astype(
+        jnp.bfloat16
+    )
+    for target in others:
+        sides_copy(col, target).start()
+
+    @pl.when(is_owner)
+    def _():
+        right_all[row % owners, col] = right_own[...]
+
+    for source in others:
+        sides_copy(source, source).wait_recv()
+    for index in range(cols):
+        left_ref[index * piece : (index + 1) * piece] = sides[index]
+    for slot in range(owners):
+        for index in range(cols):
+
+            @pl.when(jnp.logical_or(row != col * owners + slot, col != index))
+            def _():
+                right_copy(slot, index, 1).wait_recv()
+
+            start_row = slot * count + index * piece
+            right_ref[start_row : start_row + piece] = right_all[slot, index]
+
+    for chunk in range(2):
+        pass_on(row, chunk, True, True, finish)
+        for step in range(1, chips - 1):
+
+            @pl.when(chip - step >= 0)
+            def _():
+                pass_on(row - 2 * step, chunk, step < chips - 2, False, finish)
+
+            @pl.when(chip + step < chips)
+            def _():
+                pass_on(row + 2 * step, chunk, False, step < chips - 2, finish)
+
+    @pl.when(outer)
+    def _():
+        for part in range(2):
+            pass_on(farthest, part, False, False, finish)
+            far_out(part).wait_send()
+            share(part, finish)
+            share_corner(part, finish)
+
+    rel_copy(slots - 2).wait()
+    rel_copy(slots - 1).wait()
+    for target in others:
+        out_copy(col, target).wait_send()
+        stat_copy(col, target).wait_send()
+        single_copy(col, target).wait_send()
+        sides_copy(col, target).wait_send()
+        gain_copy(col, target).wait_send()
+
+    for step in range(1, rows):
+        right_copy(row % owners, col, step).wait_send()
+
+    @pl.when(jnp.logical_not(is_owner))
+    def _():
+        right_copy(row % owners, col, 0).wait_send()
+
+
 def padded(array, axis, size, groups=1):
     width = array.shape[axis] // groups
     if width == size:
@@ -506,9 +1111,8 @@
     return array.reshape(shape[:axis] + (groups * size,) + shape[axis + 1 :])
 
 
-def local(
+def front_general(
     hidden,
-    rel_bins,
     attn_gain,
     w_query,
     w_key,
@@ -519,10 +1123,6 @@
     w_second,
     w_left,
     w_right,
-    rel_table,
-    pair_gain,
-    w_expand,
-    w_contract,
 ):
     rows = lax.axis_size("row")
     cols = lax.axis_size("col")
@@ -556,7 +1156,7 @@
     bf16 = jnp.bfloat16
     f32 = jnp.float32
     dma = pltpu.SemaphoreType.DMA
-    left, right = pl.pallas_call(
+    return pl.pallas_call(
         functools.partial(front_kernel, rows, cols, model_width),
         out_shape=(
             jax.ShapeDtypeStruct((count, channels), bf16),
@@ -610,6 +1210,201 @@
         w_left,
         w_right,
     )
+
+
+def spelled_kernel(rel_ref, left_ref, right_ref, gain_ref, expand_ref, contract_ref, out_ref):
+    block_rows, col_count, channels = rel_ref.shape
+    right = right_ref[...].astype(jnp.float32)
+    pair_in = jnp.concatenate(
+        [
+            rel_ref[i].astype(jnp.float32) + (right + left_ref[i : i + 1, :].astype(jnp.float32))
+            for i in range(block_rows)
+        ],
+        0,
+    )
+    average = jnp.sum(pair_in, -1, keepdims=True) / channels
+    variance = jnp.sum(pair_in * pair_in, -1, keepdims=True) / channels - average * average
+    normed = ((pair_in - average) * lax.rsqrt(variance + epsilon) * gain_ref[...]).astype(
+        jnp.bfloat16
+    )
+    expanded = jnp.dot(normed, expand_ref[...], preferred_element_type=jnp.float32)
+    expanded = jnp.maximum(expanded.astype(jnp.bfloat16), 0)
+    update = jnp.dot(expanded, contract_ref[...], preferred_element_type=jnp.float32)
+    out_ref[...] = (pair_in + update).astype(out_ref.dtype).reshape(out_ref.shape)
+
+
+def spelled_stage(rel, left, right, pair_gain, w_expand, w_contract):
+    row_count, col_count, channels = rel.shape
+    block_rows = math.gcd(row_count, 32)
+    whole = lambda array: pl.BlockSpec(array.shape, lambda i: (0, 0))
+    gain = pair_gain.reshape(1, channels)
+    tile = pl.BlockSpec((block_rows, col_count, channels), lambda i: (i, 0, 0))
+    return pl.pallas_call(
+        spelled_kernel,
+        grid=(row_count // block_rows,),
+        in_specs=[
+            tile,
+            pl.BlockSpec((block_rows, channels), lambda i: (i, 0)),
+            whole(right),
+            whole(gain),
+            whole(w_expand),
+            whole(w_contract),
+        ],
+        out_specs=tile,
+        out_shape=jax.ShapeDtypeStruct(rel.shape, jnp.bfloat16),
+        compiler_params=pltpu.CompilerParams(
+            dimension_semantics=("arbitrary",), vmem_limit_bytes=56 << 20
+        ),
+    )(rel, left, right, gain, w_expand, w_contract)
+
+
+def front_plane(
+    hidden,
+    attn_gain,
+    w_query,
+    w_key,
+    w_value,
+    w_out,
+    final_gain,
+    w_single,
+    w_second,
+    w_left,
+    w_right,
+    rel_bins,
+    rel_table,
+):
+    rows = lax.axis_size("row")
+    cols = lax.axis_size("col")
+    count, model_width = hidden.shape
+    width = -(-w_query.shape[1] // 128) * 128
+    features = -(-w_single.shape[0] // 128) * 128
+    pairs = width // 128
+    piece = count // cols
+    owners = rows // cols
+    single_width = w_second.shape[0]
+    channels = w_left.shape[1]
+    frequency = np.exp(np.arange(HD // 2) * (-2.0 * math.log(10000.0) / HD))
+    frequency = np.concatenate([frequency] * 4)[None, :]
+    offsets = np.arange(count)[:, None] * frequency
+    steps = (np.arange(rows) * count)[:, None] * frequency
+    angles = [
+        jnp.asarray(turn(angle), jnp.float32)
+        for angle in (offsets, steps)
+        for turn in (np.cos, np.sin)
+    ]
+    weights = (w_query, w_key, w_value, w_out, w_single, w_second)
+    vmem = pl.BlockSpec(memory_space=pltpu.VMEM)
+    anywhere = pl.BlockSpec(memory_space=pl.ANY)
+    bf16 = jnp.bfloat16
+    f32 = jnp.float32
+    dma = pltpu.SemaphoreType.DMA
+    return pl.pallas_call(
+        functools.partial(plane_kernel, rows, cols, model_width),
+        out_shape=(
+            jax.ShapeDtypeStruct((count, channels), bf16),
+            jax.ShapeDtypeStruct((owners * count, channels), bf16),
+            jax.ShapeDtypeStruct(rel_bins.shape + (channels,), bf16),
+        ),
+        in_specs=[vmem, anywhere] + [vmem] * 6 + [anywhere] * 6 + [vmem] * 4,
+        out_specs=(vmem, vmem, anywhere),
+        scratch_shapes=[pltpu.VMEM(weight.shape, bf16) for weight in weights]
+        + [
+            pltpu.VMEM((count, features), bf16),
+            pltpu.VMEM((2, piece // 2, model_width), bf16),
+            pltpu.VMEM((cols, 2, piece // 2, model_width), bf16),
+            pltpu.VMEM((rows, 2, pairs, count, 128), bf16),
+            pltpu.VMEM((pairs, 2 * count, 128), bf16),
+            pltpu.VMEM((pairs, 2 * count, count), f32),
+            pltpu.VMEM((pairs, 2 * count, 128), f32),
+            pltpu.VMEM((count, width), bf16),
+            pltpu.VMEM((cols, count, features), bf16),
+            pltpu.VMEM((cols, count, features), bf16),
+            pltpu.VMEM((cols, piece, 128), f32),
+            pltpu.VMEM((cols, piece, 128), f32),
+            pltpu.VMEM((cols, 8, single_width), f32),
+            pltpu.VMEM((cols, piece, single_width), f32),
+            pltpu.VMEM((cols, piece, single_width), bf16),
+            pltpu.VMEM((cols, piece, single_width), bf16),
+            pltpu.VMEM((cols, piece, channels), bf16),
+            pltpu.VMEM((piece, channels), bf16),
+            pltpu.VMEM((owners, cols, piece, channels), bf16),
+            pltpu.VMEM((-(-rel_table.shape[0] // 128) * 128, channels), bf16),
+            pltpu.VMEM((2, rel_bins.shape[0] // 8, rel_bins.shape[1], channels), bf16),
+            dma((7,)),
+            dma((2,)),
+            dma((3, 2)),
+            dma((cols, 2)),
+            dma((3, rows, 2)),
+            dma((rows, 2)),
+            dma((cols,)),
+            dma((cols,)),
+            dma((cols,)),
+            dma((cols,)),
+            dma((cols,)),
+            dma((cols,)),
+            dma((cols,)),
+            dma((cols,)),
+            dma((rows,)),
+            dma((owners, cols)),
+            dma((cols,)),
+            dma((cols,)),
+            dma((2,)),
+        ],
+        compiler_params=pltpu.CompilerParams(
+            collective_id=0, has_side_effects=True, vmem_limit_bytes=56 << 20
+        ),
+    )(
+        hidden,
+        hidden,
+        attn_gain,
+        *angles,
+        final_gain,
+        *weights,
+        w_left,
+        w_right,
+        rel_bins,
+        rel_table,
+    )
+
+
+def local(
+    hidden,
+    rel_bins,
+    attn_gain,
+    w_query,
+    w_key,
+    w_value,
+    w_out,
+    final_gain,
+    w_single,
+    w_second,
+    w_left,
+    w_right,
+    rel_table,
+    pair_gain,
+    w_expand,
+    w_contract,
+):
+    rows = lax.axis_size("row")
+    cols = lax.axis_size("col")
+    aligned = w_query.shape[1] % 128 == 0 and hidden.shape[0] % (32 * cols) == 0
+    operands = (
+        hidden,
+        attn_gain,
+        w_query,
+        w_key,
+        w_value,
+        w_out,
+        final_gain,
+        w_single,
+        w_second,
+        w_left,
+        w_right,
+    )
+    if rows == 2 * cols and cols == 4 and aligned:
+        left, right, rel = front_plane(*operands, rel_bins, rel_table)
+        return spelled_stage(rel, left, right, pair_gain, w_expand, w_contract)
+    left, right = front_general(*operands)
     return pair_stage(rel_bins, left, right, rel_table, pair_gain, w_expand, w_contract)
 
 

time: 80.6 us -> 74.7 us (0.927)
  Pallas kernels: 79.3 us -> 74.6 us
  other arithmetic: 1.14 us -> 0 us
    pallas_call x2, Pallas kernels: 79.3 us -> 74.6 us  [the longest x1 52.8 us: front_plane(): pl.pallas_call(functools.partial(plane_kernel, rows, cols, model_width),...]
    concatenate x1 -> x0, other arithmetic: 0.81 us -> none  [local(): cosine = jnp.concatenate([cosine] * 4, -1)]
where the time goes in v1:
time: 74.7 us; the launch traced here: 74.6 us
  Pallas kernels  74.6 us (100%)
    pallas_call x1, Pallas kernels, front_plane(): pl.pallas_call(functools.partial(plane_kernel, rows, cols, model_width),...  52.8 us
    pallas_call x1, Pallas kernels, spelled_stage(): pl.pallas_call(spelled_kernel, grid=(row_count // block_rows,), in_specs=...  21.8 us

profile of v1, /device:TPU:0, one launch (start us, length us, event | category | flops | bytes accessed | tf_op | source)
XLA Modules:
  0.0 74.6 jit_solution(15883943524927234180)
XLA Ops:
  0.0 52.8 %shard_map.190 = (bf16[128,128]{1,0:T(8,128)(2,1)}, bf16[256,128]{1,0:T(8,128)(2,1)}, bf16[128,256,128]{2,1,0:T(8,128)(2,1)}) custom-call(bf16[128,2560]{1,0:T(8,128)(2,1)} %own_hbm.1, bf16[128,2560]{1,0:T(8,128)(2,1)} %own_hbm.1, f32[2560]{0:T(1024)} %attn_gain_ref.1, f32[128,128]{1,0:T(8,128)} %constant.8.clone.cos_ref, f32[128,128]{1,0:T(8,128)} %constant.9.clone.sin_ref, ...), custom_call_target="tpu_custom_call" | custom-call | tf_op jit(solution)/shard_map/pallas_call | solution.py:1301
  52.8 21.8 %shard_map.191 = bf16[128,256,128]{2,1,0:T(8,128)(2,1)} custom-call(bf16[128,256,128]{2,1,0:T(8,128)(2,1)} %get-tuple-element.8.rel_ref, bf16[128,128]{1,0:T(8,128)(2,1)} %get-tuple-element.9.left_ref, bf16[256,128]{1,0:T(8,128)(2,1)} %get-tuple-element.10.right_ref, f32[1,128]{1,0:T(1,128)} %bitcast.1, bf16[128,512]{1,0:T(8,128)(2,1)} %expand_ref.1, ...), custom_call_target="tpu_custom_call" | custom-call | tf_op jit(solution)/shard_map/pallas_call | solution.py:1242

commit v2 on v1

--- a/solution.py
+++ b/solution.py
@@ -532,7 +532,9 @@
     kv,
     query,
     totals,
+    shares,
     numerator,
+    w_sides,
     context,
     out_send,
     out_recv,
@@ -738,13 +740,6 @@
     def finish(copy):
         copy.wait_send()
 
-    pl.semaphore_wait(barrier, greetings)
-
-    @pl.when(outer)
-    def _():
-        for part in range(2):
-            far_out(part).start()
-
     def keys_of(rows_in, source):
         cosine, sine = tables(source)
         projected = jnp.dot(rows_in, w_key[...], preferred_element_type=jnp.float32)
@@ -758,6 +753,13 @@
         for pair in range(pairs):
             kv[source, 1, pair] = projected[:, pair * 128 : pair * 128 + 128].astype(jnp.bfloat16)
 
+    pl.semaphore_wait(barrier, greetings)
+
+    @pl.when(outer)
+    def _():
+        for part in range(2):
+            far_out(part).start()
+
     attn_in = normalize(hidden_ref[...])
     loads[0].wait()
     keys_of(attn_in, row)
@@ -765,12 +767,6 @@
     loads[1].wait()
     values_of(attn_in, row)
     pass_on(row, 1, True, True, start)
-
-    @pl.when(outer)
-    def _():
-        for part in range(2):
-            far_wait(col, part)
-            share(part, start)
 
     def gain_copy(source, target):
         return pltpu.make_async_remote_copy(
@@ -829,27 +825,32 @@
     totals[...] = jnp.zeros_like(totals)
     numerator[...] = jnp.zeros_like(numerator)
 
-    def attend(source):
+    def score(source, slot):
         for pair in range(pairs):
-            scores = lax.dot_general(
-                query[pair],
-                kv[source, 0, pair],
-                (((1,), (1,)), ((), ())),
-                preferred_element_type=jnp.float32,
+            keys = kv[pl.ds(2 * source, 2), 0, pair].reshape(2 * count, 128)
+            weights = jnp.exp(
+                lax.dot_general(
+                    query[pair],
+                    keys,
+                    (((1,), (1,)), ((), ())),
+                    preferred_element_type=jnp.float32,
+                )
             )
-            weights = jnp.exp(scores)
-            totals[pair] += weights
+            totals[pair] += weights[:, :count] + weights[:, count:]
+            shares[slot, pair] = weights.astype(jnp.bfloat16)
+
+    def mix(source, slot):
+        for pair in range(pairs):
+            values = kv[pl.ds(2 * source, 2), 1, pair].reshape(2 * count, 128)
             numerator[pair] += jnp.dot(
-                weights.astype(jnp.bfloat16),
-                kv[source, 1, pair],
-                preferred_element_type=jnp.float32,
+                shares[slot, pair], values, preferred_element_type=jnp.float32
             )
 
-    def arrive(source):
-        for chunk in range(2):
-            kv_copy(source, chunk, 2, partner).wait_recv()
-
-    attend(row)
+    def arrive(source, chunk):
+        kv_copy(source, chunk, 2, partner).wait_recv()
+
+    arrive(partner, 0)
+    score(chip, 0)
     loads[4].wait()
     gain = final_gain_ref[...].reshape(1, -1)
     coarse = gain.astype(jnp.bfloat16)
@@ -860,6 +861,20 @@
     for target in others:
         gain_copy(col, target).start()
 
+    arrive(partner, 1)
+    mix(chip, 0)
+
+    early = jnp.where(outer, slots, 4)
+    spell(0, 2)
+
+    @pl.when(outer)
+    def _():
+        for part in range(2):
+            far_wait(col, part)
+            share(part, start)
+
+    spell(2, early)
+
     @pl.when(outer)
     def _():
         far_wait(side, 0)
@@ -867,43 +882,51 @@
         far_wait(across, 1)
         share_corner(1, start)
 
-    arrive(partner)
-    attend(partner)
-    spell(0, slots // 2)
 
     def near(step, onward):
         from_left = chip - step >= 0
         from_right = chip + step < chips
-        for chunk in range(2):
-
+
+        def receive(chunk):
             @pl.when(from_left)
             def _():
-                source = row - 2 * step
-                kv_copy(source, chunk, 2, partner).wait_recv()
-                pass_on(source, chunk, onward, False, start)
+                arrive(row - 2 * step, chunk)
+                pass_on(row - 2 * step, chunk, onward, False, start)
 
             @pl.when(from_right)
             def _():
-                source = row + 2 * step
-                kv_copy(source, chunk, 2, partner).wait_recv()
-                pass_on(source, chunk, False, onward, start)
-
-        @pl.when(from_left)
-        def _():
-            attend(row - 2 * step)
-            arrive(partner - 2 * step)
-            attend(partner - 2 * step)
-
-        @pl.when(from_right)
-        def _():
-            attend(row + 2 * step)
-            arrive(partner + 2 * step)
-            attend(partner + 2 * step)
+                arrive(row + 2 * step, chunk)
+                pass_on(row + 2 * step, chunk, False, onward, start)
+
+        def use(chunk):
+            @pl.when(from_left)
+            def _():
+                arrive(partner - 2 * step, chunk)
+                (mix if chunk else score)(chip - step, 0)
+
+            @pl.when(from_right)
+            def _():
+                arrive(partner + 2 * step, chunk)
+                (mix if chunk else score)(chip + step, 1)
+
+        receive(0)
+        if onward:
+            receive(1)
+        use(0)
+        if not onward:
+            receive(1)
+        use(1)
 
     for step in range(1, chips - 1):
         near(step, step < chips - 2)
         if step == 1:
-            spell(slots // 2, slots)
+            loads[5].wait()
+            w_sides[...] = jnp.dot(
+                w_second[...],
+                jnp.concatenate([w_left_ref[...], w_right_ref[...]], 1),
+                preferred_element_type=jnp.float32,
+            ).astype(jnp.bfloat16)
+            spell(early, slots)
 
             @pl.when(outer)
             def _():
@@ -916,23 +939,28 @@
                 pass_on(farthest, 0, False, False, start)
                 values_of(rows_in, farthest)
                 pass_on(farthest, 1, False, False, start)
-                other = farthest + partner - row
-                attend(farthest)
-                arrive(other)
-                attend(other)
+                for chunk in range(2):
+                    arrive(farthest + partner - row, chunk)
+                    (mix if chunk else score)(chips - 1 - chip, 0)
+
 
     for pair in range(pairs):
-        shares = numerator[pair] / jnp.sum(totals[pair], -1, keepdims=True)
+        mixed = numerator[pair] / jnp.sum(totals[pair], -1, keepdims=True)
         context[:, pair * 128 : pair * 128 + 128] = jnp.where(
-            first_head, shares[:count], shares[count:]
+            first_head, mixed[:count], mixed[count:]
         ).astype(jnp.bfloat16)
 
-    def out_copy(source, target):
+    split = count // 2
+    halves = [slice(0, split), slice(split, count)]
+    firsts = (side, across)
+    seconds = (across, side)
+
+    def out_copy(slot, target):
         return pltpu.make_async_remote_copy(
-            src_ref=out_send.at[target],
-            dst_ref=out_recv.at[source],
-            send_sem=out_send_sem.at[target],
-            recv_sem=out_recv_sem.at[source],
+            src_ref=out_send.at[slot],
+            dst_ref=out_recv.at[slot],
+            send_sem=out_send_sem.at[slot],
+            recv_sem=out_recv_sem.at[slot],
             device_id=(row, target),
             device_id_type=MESH,
         )
@@ -942,14 +970,32 @@
         return jnp.dot(context[...], w_out[:, columns], preferred_element_type=jnp.float32)
 
     loads[3].wait()
-    for target in others:
-        out_send[target] = out_part(target).astype(jnp.bfloat16)
-        out_copy(col, target).start()
+    passing = out_part(corner).astype(jnp.bfloat16)
+    for half in range(2):
+        out_send[half] = passing[halves[half]]
+        out_copy(half, firsts[half]).start()
+    kept = [None, None]
+    for half in range(2):
+        passing = out_part(firsts[half])
+        out_send[2 + half] = passing[halves[half]].astype(jnp.bfloat16)
+        out_copy(2 + half, firsts[half]).start()
+        kept[1 - half] = passing[halves[1 - half]]
+    for half in range(2):
+        out_copy(half, firsts[half]).wait_recv()
+        out_send[4 + half] = (kept[half] + out_recv[half].astype(jnp.float32)).astype(jnp.bfloat16)
+        out_copy(4 + half, seconds[half]).start()
     loads[6].wait()
     resid = own[...].astype(jnp.float32) + out_part(col)
-    for source in others:
-        out_copy(source, source).wait_recv()
-        resid += out_recv[source].astype(jnp.float32)
+    collected = []
+    for half in range(2):
+        out_copy(2 + half, firsts[half]).wait_recv()
+        out_copy(4 + half, seconds[half]).wait_recv()
+        collected.append(
+            resid[halves[half]]
+            + out_recv[2 + half].astype(jnp.float32)
+            + out_recv[4 + half].astype(jnp.float32)
+        )
+    resid = jnp.concatenate(collected, 0)
 
     def stat_copy(source, target):
         return pltpu.make_async_remote_copy(
@@ -1004,9 +1050,8 @@
         single_copy(source, source).wait_recv()
         summed += single_recv[source].astype(jnp.float32)
     lifted = jnp.maximum(summed * scale, 0.0).astype(jnp.bfloat16)
-    loads[5].wait()
-    single = jnp.dot(lifted, w_second[...], preferred_element_type=jnp.float32)
-    single = single.astype(jnp.bfloat16)
+    channels = w_left_ref.shape[1]
+    both = jnp.dot(lifted, w_sides[...], preferred_element_type=jnp.float32).astype(jnp.bfloat16)
 
     def sides_copy(source, target):
         return pltpu.make_async_remote_copy(
@@ -1028,9 +1073,7 @@
             device_id_type=MESH,
         )
 
-    right_own[...] = jnp.dot(
-        single, w_right_ref[...], preferred_element_type=jnp.float32
-    ).astype(jnp.bfloat16)
+    right_own[...] = both[:, channels:]
     for step in range(1, rows):
         right_copy(row % owners, col, step).start()
 
@@ -1038,9 +1081,7 @@
     def _():
         right_copy(row % owners, col, 0).start()
 
-    sides[col] = jnp.dot(single, w_left_ref[...], preferred_element_type=jnp.float32).astype(
-        jnp.bfloat16
-    )
+    sides[col] = both[:, :channels]
     for target in others:
         sides_copy(col, target).start()
 
@@ -1084,8 +1125,11 @@
 
     rel_copy(slots - 2).wait()
     rel_copy(slots - 1).wait()
+    for half in range(2):
+        out_copy(half, firsts[half]).wait_send()
+        out_copy(2 + half, firsts[half]).wait_send()
+        out_copy(4 + half, seconds[half]).wait_send()
     for target in others:
-        out_copy(col, target).wait_send()
         stat_copy(col, target).wait_send()
         single_copy(col, target).wait_send()
         sides_copy(col, target).wait_send()
@@ -1315,10 +1359,12 @@
             pltpu.VMEM((rows, 2, pairs, count, 128), bf16),
             pltpu.VMEM((pairs, 2 * count, 128), bf16),
             pltpu.VMEM((pairs, 2 * count, count), f32),
+            pltpu.VMEM((2, pairs, 2 * count, 2 * count), bf16),
             pltpu.VMEM((pairs, 2 * count, 128), f32),
+            pltpu.VMEM((single_width, 2 * channels), bf16),
             pltpu.VMEM((count, width), bf16),
-            pltpu.VMEM((cols, count, features), bf16),
-            pltpu.VMEM((cols, count, features), bf16),
+            pltpu.VMEM((6, count // 2, features), bf16),
+            pltpu.VMEM((6, count // 2, features), bf16),
             pltpu.VMEM((cols, piece, 128), f32),
             pltpu.VMEM((cols, piece, 128), f32),
             pltpu.VMEM((cols, 8, single_width), f32),
@@ -1328,7 +1374,7 @@
             pltpu.VMEM((cols, piece, channels), bf16),
             pltpu.VMEM((piece, channels), bf16),
             pltpu.VMEM((owners, cols, piece, channels), bf16),
-            pltpu.VMEM((-(-rel_table.shape[0] // 128) * 128, channels), bf16),
+            pltpu.VMEM((-(-rel_table.shape[0] // 16) * 16, channels), bf16),
             pltpu.VMEM((2, rel_bins.shape[0] // 8, rel_bins.shape[1], channels), bf16),
             dma((7,)),
             dma((2,)),
@@ -1336,8 +1382,8 @@
             dma((cols, 2)),
             dma((3, rows, 2)),
             dma((rows, 2)),
-            dma((cols,)),
-            dma((cols,)),
+            dma((6,)),
+            dma((6,)),
             dma((cols,)),
             dma((cols,)),
             dma((cols,)),

time: 74.7 us -> 70 us (0.937)
  Pallas kernels: 74.6 us -> 69.9 us
    pallas_call x1, Pallas kernels: 52.8 us -> 48.1 us  [front_plane(): pl.pallas_call(functools.partial(plane_kernel, rows, cols, model_width),...]
where the time goes in v2:
time: 70 us; the launch traced here: 69.9 us
  Pallas kernels  69.9 us (100%)
    pallas_call x1, Pallas kernels, front_plane(): pl.pallas_call(functools.partial(plane_kernel, rows, cols, model_width),...  48.1 us
    pallas_call x1, Pallas kernels, spelled_stage(): pl.pallas_call(spelled_kernel, grid=(row_count // block_rows,), in_specs=...  21.8 us

profile of v2, /device:TPU:0, one launch (start us, length us, event | category | flops | bytes accessed | tf_op | source)
XLA Modules:
  0.0 69.9 jit_solution(3116519400329036074)
XLA Ops:
  0.0 48.1 %shard_map.190 = (bf16[128,128]{1,0:T(8,128)(2,1)}, bf16[256,128]{1,0:T(8,128)(2,1)}, bf16[128,256,128]{2,1,0:T(8,128)(2,1)}) custom-call(bf16[128,2560]{1,0:T(8,128)(2,1)} %own_hbm.1, bf16[128,2560]{1,0:T(8,128)(2,1)} %own_hbm.1, f32[2560]{0:T(1024)} %attn_gain_ref.1, f32[128,128]{1,0:T(8,128)} %constant.8.clone.cos_ref, f32[128,128]{1,0:T(8,128)} %constant.9.clone.sin_ref, ...), custom_call_target="tpu_custom_call" | custom-call | tf_op jit(solution)/shard_map/pallas_call | solution.py:1345
  48.1 21.8 %shard_map.191 = bf16[128,256,128]{2,1,0:T(8,128)(2,1)} custom-call(bf16[128,256,128]{2,1,0:T(8,128)(2,1)} %get-tuple-element.8.rel_ref, bf16[128,128]{1,0:T(8,128)(2,1)} %get-tuple-element.9.left_ref, bf16[256,128]{1,0:T(8,128)(2,1)} %get-tuple-element.10.right_ref, f32[1,128]{1,0:T(1,128)} %bitcast.1, bf16[128,512]{1,0:T(8,128)(2,1)} %expand_ref.1, ...), custom_call_target="tpu_custom_call" | custom-call | tf_op jit(solution)/shard_map/pallas_call | solution.py:1286

commit v3 on v2

--- a/solution.py
+++ b/solution.py
@@ -613,28 +613,20 @@
 
     greet(partner, col)
 
+    @pl.when(chip + 1 < chips)
+    def _():
+        greet(row + 2, col)
+
+    @pl.when(chip >= 1)
+    def _():
+        greet(row - 2, col)
+
     @pl.when(outer)
     def _():
         greet(farthest, col)
 
-    @pl.when(chip + 1 < chips)
-    def _():
-        greet(row + 2, col)
-
-    @pl.when(chip >= 1)
-    def _():
-        greet(row - 2, col)
-
-    for slot in range(owners):
-        for index in range(cols):
-
-            @pl.when(jnp.logical_or(row != col * owners + slot, col != index))
-            def _():
-                greet(col * owners + slot, index)
-
-    greetings = cols + rows + jnp.where(outer, 1, 0)
+    greetings = cols + jnp.where(outer, 1, 0)
     greetings += jnp.where(chip + 1 < chips, 1, 0) + jnp.where(chip >= 1, 1, 0)
-    greetings -= jnp.where(is_owner, 1, 0)
     for step in range(1, cols):
         pl.semaphore_signal(
             barrier, inc=1, device_id=(row, (col + step) % cols), device_id_type=MESH

time: 70 us -> 68.9 us (0.984)
  Pallas kernels: 69.9 us -> 68.7 us
    pallas_call x1, Pallas kernels: 48.1 us -> 46.9 us  [front_plane(): pl.pallas_call(functools.partial(plane_kernel, rows, cols, model_width),...]
where the time goes in v3:
time: 68.9 us; the launch traced here: 68.7 us
  Pallas kernels  68.7 us (100%)
    pallas_call x1, Pallas kernels, front_plane(): pl.pallas_call(functools.partial(plane_kernel, rows, cols, model_width),...  46.9 us
    pallas_call x1, Pallas kernels, spelled_stage(): pl.pallas_call(spelled_kernel, grid=(row_count // block_rows,), in_specs=...  21.8 us

profile of v3, /device:TPU:0, one launch (start us, length us, event | category | flops | bytes accessed | tf_op | source)
XLA Modules:
  0.0 68.7 jit_solution(8521376934349454927)
XLA Ops:
  0.0 46.9 %shard_map.190 = (bf16[128,128]{1,0:T(8,128)(2,1)}, bf16[256,128]{1,0:T(8,128)(2,1)}, bf16[128,256,128]{2,1,0:T(8,128)(2,1)}) custom-call(bf16[128,2560]{1,0:T(8,128)(2,1)} %own_hbm.1, bf16[128,2560]{1,0:T(8,128)(2,1)} %own_hbm.1, f32[2560]{0:T(1024)} %attn_gain_ref.1, f32[128,128]{1,0:T(8,128)} %constant.8.clone.cos_ref, f32[128,128]{1,0:T(8,128)} %constant.9.clone.sin_ref, ...), custom_call_target="tpu_custom_call" | custom-call | tf_op jit(solution)/shard_map/pallas_call | solution.py:1337
  47.0 21.8 %shard_map.191 = bf16[128,256,128]{2,1,0:T(8,128)(2,1)} custom-call(bf16[128,256,128]{2,1,0:T(8,128)(2,1)} %get-tuple-element.8.rel_ref, bf16[128,128]{1,0:T(8,128)(2,1)} %get-tuple-element.9.left_ref, bf16[256,128]{1,0:T(8,128)(2,1)} %get-tuple-element.10.right_ref, f32[1,128]{1,0:T(1,128)} %bitcast.1, bf16[128,512]{1,0:T(8,128)(2,1)} %expand_ref.1, ...), custom_call_target="tpu_custom_call" | custom-call | tf_op jit(solution)/shard_map/pallas_call | solution.py:1278

commit v4 on v3

--- a/solution.py
+++ b/solution.py
@@ -10,6 +10,9 @@
 from jax.sharding import PartitionSpec as P
 
 HD = 64
+SUB = 8
+CHUNKS = 8
+WINDOW = 3
 MESH = pl.DeviceIdType.MESH
 
 
@@ -520,6 +523,7 @@
     left_ref,
     right_ref,
     rel_hbm,
+    flags_ref,
     w_query,
     w_key,
     w_value,
@@ -770,7 +774,7 @@
             device_id_type=MESH,
         )
 
-    others = [(col + step) % cols for step in range(1, cols)]
+    others = [corner, side, across]
     loads[2].wait()
     cosine, sine = tables(row)
     projected = jnp.dot(attn_in, w_query[...], preferred_element_type=jnp.float32) * HD ** (-0.5)
@@ -856,6 +860,18 @@
     arrive(partner, 1)
     mix(chip, 0)
 
+    grouped = bins_ref[...].reshape(flags_ref.shape[0], -1, col_count)
+    high = jnp.max(grouped, 1)
+    low = jnp.min(grouped, 1)
+    spot = lax.broadcasted_iota(jnp.int32, flags_ref.shape, 1)
+    flags = jnp.full(flags_ref.shape, -1, jnp.int32)
+    width = col_count // CHUNKS
+    for index in range(CHUNKS):
+        span = slice(index * width, (index + 1) * width)
+        top = jnp.max(high[:, span], -1, keepdims=True)
+        bottom = jnp.min(low[:, span], -1, keepdims=True)
+        flags = jnp.where(spot == index, jnp.where(top == bottom, top, -1), flags)
+    flags_ref[...] = flags
     early = jnp.where(outer, slots, 4)
     spell(0, 2)
 
@@ -1248,50 +1264,176 @@
     )
 
 
-def spelled_kernel(rel_ref, left_ref, right_ref, gain_ref, expand_ref, contract_ref, out_ref):
-    block_rows, col_count, channels = rel_ref.shape
-    right = right_ref[...].astype(jnp.float32)
-    pair_in = jnp.concatenate(
-        [
-            rel_ref[i].astype(jnp.float32) + (right + left_ref[i : i + 1, :].astype(jnp.float32))
-            for i in range(block_rows)
-        ],
-        0,
-    )
-    average = jnp.sum(pair_in, -1, keepdims=True) / channels
-    variance = jnp.sum(pair_in * pair_in, -1, keepdims=True) / channels - average * average
-    normed = ((pair_in - average) * lax.rsqrt(variance + epsilon) * gain_ref[...]).astype(
-        jnp.bfloat16
-    )
-    expanded = jnp.dot(normed, expand_ref[...], preferred_element_type=jnp.float32)
-    expanded = jnp.maximum(expanded.astype(jnp.bfloat16), 0)
-    update = jnp.dot(expanded, contract_ref[...], preferred_element_type=jnp.float32)
-    out_ref[...] = (pair_in + update).astype(out_ref.dtype).reshape(out_ref.shape)
-
-
-def spelled_stage(rel, left, right, pair_gain, w_expand, w_contract):
-    row_count, col_count, channels = rel.shape
+def banded_kernel(
+    flags,
+    rel_ref,
+    left_ref,
+    right_ref,
+    table_ref,
+    gain_ref,
+    expand_ref,
+    contract_ref,
+    out_ref,
+    table,
+    left_parts,
+    right_parts,
+    table_parts,
+    left_wide,
+    right_wide,
+    table_wide,
+):
+    block_rows, col_count, channels = out_ref.shape
+    bins = table_ref.shape[0]
+    chunk = col_count // CHUNKS
+    width = WINDOW * chunk
+    sub = SUB
+
+    @pl.when(pl.program_id(0) == 0)
+    def _():
+        table[...] = jnp.zeros_like(table)
+        table[:bins] = table_ref[...]
+        gain = gain_ref[...]
+        weights = jnp.concatenate([expand_ref[...]] * 2, 0)
+        for source, parts, wide in (
+            (left_ref, left_parts, left_wide),
+            (right_ref, right_parts, right_wide),
+            (table, table_parts, table_wide),
+        ):
+            values = source[...].astype(jnp.float32)
+            centred = values - jnp.sum(values, -1, keepdims=True) / channels
+            parts[0] = values
+            parts[1] = centred
+            scaled = centred * gain
+            coarse = scaled.astype(jnp.bfloat16)
+            fine = (scaled - coarse.astype(jnp.float32)).astype(jnp.bfloat16)
+            wide[...] = jnp.dot(
+                jnp.concatenate([coarse, fine], 1), weights, preferred_element_type=jnp.float32
+            )
+
+    gain = gain_ref[...]
+
+    def block(first, local, group, start, mixed_width, places):
+        sums = []
+        scales = []
+        expanded = []
+        targets = []
+        if mixed_width:
+            right = right_parts[0, pl.ds(start, mixed_width)]
+            pair_in = jnp.concatenate(
+                [
+                    rel_ref[local + i, pl.ds(start, mixed_width)].astype(jnp.float32)
+                    + (right + left_parts[0, pl.ds(first + i, 1)])
+                    for i in range(sub)
+                ],
+                0,
+            )
+            average = jnp.sum(pair_in, -1, keepdims=True) / channels
+            variance = (
+                jnp.sum(pair_in * pair_in, -1, keepdims=True) / channels - average * average
+            )
+            normed = ((pair_in - average) * lax.rsqrt(variance + epsilon) * gain).astype(
+                jnp.bfloat16
+            )
+            wide = jnp.dot(normed, expand_ref[...], preferred_element_type=jnp.float32)
+            wide = jnp.maximum(wide.astype(jnp.bfloat16), 0)
+            for i in range(sub):
+                rows = slice(i * mixed_width, (i + 1) * mixed_width)
+                targets.append((local + i, start, mixed_width))
+                sums.append(pair_in[rows])
+                scales.append(None)
+                expanded.append(wide[rows])
+        for place in places:
+            begin = pl.multiple_of(place * chunk, chunk)
+            span = pl.ds(begin, chunk)
+            spot = pl.ds(flags[group, place], 1)
+            right = right_parts[0, span]
+            right_centred = right_parts[1, span]
+            right_up = right_wide[span]
+            for i in range(sub):
+                one = pl.ds(first + i, 1)
+                base = left_parts[0, one] + table_parts[0, spot]
+                base_centred = left_parts[1, one] + table_parts[1, spot]
+                base_up = left_wide[one] + table_wide[spot]
+                centred = right_centred + base_centred
+                variance = jnp.sum(centred * centred, -1, keepdims=True) / channels
+                targets.append((local + i, begin, chunk))
+                scales.append(lax.rsqrt(variance + epsilon))
+                sums.append(right + base)
+                expanded.append(jnp.maximum((right_up + base_up).astype(jnp.bfloat16), 0))
+        update = jnp.dot(
+            jnp.concatenate(expanded, 0), contract_ref[...], preferred_element_type=jnp.float32
+        )
+        row = 0
+        for total, scale, (place, begin, size) in zip(sums, scales, targets):
+            piece = update[row : row + size]
+            if scale is not None:
+                piece = piece * scale
+            out_ref[place, pl.ds(begin, size)] = (total + piece).astype(out_ref.dtype)
+            row += size
+
+    @pl.loop(0, block_rows // sub)
+    def _(step):
+        local = pl.multiple_of(step * sub, sub)
+        first = pl.multiple_of(pl.program_id(0) * block_rows + local, sub)
+        group = pl.program_id(0) * (block_rows // sub) + step
+        begin = jnp.int32(CHUNKS)
+        end = jnp.int32(0)
+        for index in range(CHUNKS):
+            ragged = flags[group, index] < 0
+            begin = jnp.where(jnp.logical_and(ragged, begin == CHUNKS), index, begin)
+            end = jnp.where(ragged, index + 1, end)
+        none = end == 0
+        few = jnp.logical_and(end > 0, end - begin <= WINDOW)
+
+        @pl.when(none)
+        def _():
+            block(first, local, group, 0, 0, range(CHUNKS))
+
+        @pl.when(few)
+        def _():
+            window = jnp.minimum(begin, CHUNKS - WINDOW)
+            places = [
+                jnp.where(index < window, index, index + WINDOW)
+                for index in range(CHUNKS - WINDOW)
+            ]
+            block(first, local, group, pl.multiple_of(window * chunk, chunk), width, places)
+
+        @pl.when(end - begin > WINDOW)
+        def _():
+            block(first, local, group, 0, col_count, ())
+
+
+def banded_stage(flags, rel, left, right, rel_table, pair_gain, w_expand, w_contract):
+    row_count, col_count, _ = rel.shape
+    channels = right.shape[1]
+    hidden_width = w_expand.shape[1]
     block_rows = math.gcd(row_count, 32)
+    bins_padded = -(-rel_table.shape[0] // 128) * 128
     whole = lambda array: pl.BlockSpec(array.shape, lambda i: (0, 0))
     gain = pair_gain.reshape(1, channels)
+    operands = (flags, rel, left, right, rel_table, gain, w_expand, w_contract)
     tile = pl.BlockSpec((block_rows, col_count, channels), lambda i: (i, 0, 0))
+    f32 = jnp.float32
     return pl.pallas_call(
-        spelled_kernel,
+        banded_kernel,
         grid=(row_count // block_rows,),
-        in_specs=[
-            tile,
-            pl.BlockSpec((block_rows, channels), lambda i: (i, 0)),
-            whole(right),
-            whole(gain),
-            whole(w_expand),
-            whole(w_contract),
+        in_specs=[pl.BlockSpec(memory_space=pltpu.SMEM), tile]
+        + [whole(operand) for operand in operands[2:]],
+        out_specs=tile,
+        out_shape=jax.ShapeDtypeStruct((row_count, col_count, channels), jnp.bfloat16),
+        scratch_shapes=[
+            pltpu.VMEM((bins_padded, channels), jnp.bfloat16),
+            pltpu.VMEM((2, row_count, channels), f32),
+            pltpu.VMEM((2, col_count, channels), f32),
+            pltpu.VMEM((2, bins_padded, channels), f32),
+            pltpu.VMEM((row_count, hidden_width), f32),
+            pltpu.VMEM((col_count, hidden_width), f32),
+            pltpu.VMEM((bins_padded, hidden_width), f32),
         ],
-        out_specs=tile,
-        out_shape=jax.ShapeDtypeStruct(rel.shape, jnp.bfloat16),
         compiler_params=pltpu.CompilerParams(
             dimension_semantics=("arbitrary",), vmem_limit_bytes=56 << 20
         ),
-    )(rel, left, right, gain, w_expand, w_contract)
+    )(*operands)
 
 
 def front_plane(
@@ -1340,9 +1482,10 @@
             jax.ShapeDtypeStruct((count, channels), bf16),
             jax.ShapeDtypeStruct((owners * count, channels), bf16),
             jax.ShapeDtypeStruct(rel_bins.shape + (channels,), bf16),
+            jax.ShapeDtypeStruct((rel_bins.shape[0] // SUB, 128), jnp.int32),
         ),
         in_specs=[vmem, anywhere] + [vmem] * 6 + [anywhere] * 6 + [vmem] * 4,
-        out_specs=(vmem, vmem, anywhere),
+        out_specs=(vmem, vmem, anywhere, vmem),
         scratch_shapes=[pltpu.VMEM(weight.shape, bf16) for weight in weights]
         + [
             pltpu.VMEM((count, features), bf16),
@@ -1439,9 +1582,11 @@
         w_left,
         w_right,
     )
-    if rows == 2 * cols and cols == 4 and aligned:
-        left, right, rel = front_plane(*operands, rel_bins, rel_table)
-        return spelled_stage(rel, left, right, pair_gain, w_expand, w_contract)
+    if rows == 2 * cols and cols == 4 and aligned and rel_bins.shape[1] % (16 * CHUNKS) == 0:
+        left, right, rel, flags = front_plane(*operands, rel_bins, rel_table)
+        return banded_stage(
+            flags, rel, left, right, rel_table, pair_gain, w_expand, w_contract
+        )
     left, right = front_general(*operands)
     return pair_stage(rel_bins, left, right, rel_table, pair_gain, w_expand, w_contract)
 

time: 68.9 us -> 66.8 us (0.970)
  Pallas kernels: 68.7 us -> 66.7 us
    pallas_call x1, Pallas kernels: 21.8 us -> 20.3 us  [banded_stage(): pl.pallas_call(banded_kernel, grid=(row_count // block_rows,), in_specs=[...]
where the time goes in v4:
time: 66.8 us; the launch traced here: 66.7 us
  Pallas kernels  66.7 us (100%)
    pallas_call x1, Pallas kernels, front_plane(): pl.pallas_call(functools.partial(plane_kernel, rows, cols, model_width),...  46.3 us
    pallas_call x1, Pallas kernels, banded_stage(): pl.pallas_call(banded_kernel, grid=(row_count // block_rows,), in_specs=[...  20.3 us

profile of v4, /device:TPU:0, one launch (start us, length us, event | category | flops | bytes accessed | tf_op | source)
XLA Modules:
  0.0 66.7 jit_solution(11422933566484190665)
XLA Ops:
  0.0 46.3 %shard_map.190 = (bf16[128,128]{1,0:T(8,128)(2,1)}, bf16[256,128]{1,0:T(8,128)(2,1)}, bf16[128,256,128]{2,1,0:T(8,128)(2,1)}, s32[16,128]{1,0:T(8,128)}) custom-call(bf16[128,2560]{1,0:T(8,128)(2,1)} %own_hbm.1, bf16[128,2560]{1,0:T(8,128)(2,1)} %own_hbm.1, f32[2560]{0:T(1024)} %attn_gain_ref.1, f32[128,128]{1,0:T(8,128)} %constant.8.clone.cos_ref, ...), custom_call_target="tpu_custom_call" | custom-call | tf_op jit(solution)/shard_map/pallas_call | solution.py:1479
  46.3 20.3 %shard_map.191 = bf16[128,256,128]{2,1,0:T(8,128)(2,1)} custom-call(s32[16,128]{1,0:T(8,128)} %get-tuple-element.9.flags, bf16[128,256,128]{2,1,0:T(8,128)(2,1)} %get-tuple-element.10.rel_ref, bf16[128,128]{1,0:T(8,128)(2,1)} %get-tuple-element.11.left_ref, bf16[256,128]{1,0:T(8,128)(2,1)} %get-tuple-element.12.right_ref, bf16[65,128]{1,0:T(8,128)(2,1)} %table_ref.3, ...), custom_call_target="tpu_custom_call" | custom-call | tf_op jit(solution)/shard_map/pallas_call | solution.py:1417

commit v5 on v4

--- a/solution.py
+++ b/solution.py
@@ -10,7 +10,7 @@
 from jax.sharding import PartitionSpec as P
 
 HD = 64
-SUB = 8
+SUB = 16
 CHUNKS = 8
 WINDOW = 3
 MESH = pl.DeviceIdType.MESH
@@ -1407,7 +1407,7 @@
     row_count, col_count, _ = rel.shape
     channels = right.shape[1]
     hidden_width = w_expand.shape[1]
-    block_rows = math.gcd(row_count, 32)
+    block_rows = math.gcd(row_count, SUB)
     bins_padded = -(-rel_table.shape[0] // 128) * 128
     whole = lambda array: pl.BlockSpec(array.shape, lambda i: (0, 0))
     gain = pair_gain.reshape(1, channels)

time: 66.8 us -> 64.9 us (0.972)
  Pallas kernels: 66.7 us -> 64.5 us
    pallas_call x1, Pallas kernels: 20.3 us -> 18.2 us  [banded_stage(): pl.pallas_call(banded_kernel, grid=(row_count // block_rows,), in_specs=[...]
where the time goes in v5:
time: 64.9 us; the launch traced here: 64.5 us
  Pallas kernels  64.5 us (99%)
    pallas_call x1, Pallas kernels, front_plane(): pl.pallas_call(functools.partial(plane_kernel, rows, cols, model_width),...  46.3 us
    pallas_call x1, Pallas kernels, banded_stage(): pl.pallas_call(banded_kernel, grid=(row_count // block_rows,), in_specs=[...  18.2 us

profile of v5, /device:TPU:0, one launch (start us, length us, event | category | flops | bytes accessed | tf_op | source)
XLA Modules:
  0.0 64.5 jit_solution(4077477510788920354)
XLA Ops:
  0.0 46.3 %shard_map.190 = (bf16[128,128]{1,0:T(8,128)(2,1)}, bf16[256,128]{1,0:T(8,128)(2,1)}, bf16[128,256,128]{2,1,0:T(8,128)(2,1)}, s32[8,128]{1,0:T(8,128)}) custom-call(bf16[128,2560]{1,0:T(8,128)(2,1)} %own_hbm.1, bf16[128,2560]{1,0:T(8,128)(2,1)} %own_hbm.1, f32[2560]{0:T(1024)} %attn_gain_ref.1, f32[128,128]{1,0:T(8,128)} %constant.8.clone.cos_ref, ...), custom_call_target="tpu_custom_call" | custom-call | tf_op jit(solution)/shard_map/pallas_call | solution.py:1479
  46.3 18.2 %shard_map.191 = bf16[128,256,128]{2,1,0:T(8,128)(2,1)} custom-call(s32[8,128]{1,0:T(8,128)} %get-tuple-element.9.flags, bf16[128,256,128]{2,1,0:T(8,128)(2,1)} %get-tuple-element.10.rel_ref, bf16[128,128]{1,0:T(8,128)(2,1)} %get-tuple-element.11.left_ref, bf16[256,128]{1,0:T(8,128)(2,1)} %get-tuple-element.12.right_ref, bf16[65,128]{1,0:T(8,128)(2,1)} %table_ref.3, ...), custom_call_target="tpu_custom_call" | custom-call | tf_op jit(solution)/shard_map/pallas_call | solution.py:1417

commit v6 on v5

--- a/solution.py
+++ b/solution.py
@@ -1082,7 +1082,7 @@
         )
 
     right_own[...] = both[:, channels:]
-    for step in range(1, rows):
+    for step in sorted(range(1, rows), key=lambda step: abs(2 * step - rows)):
         right_copy(row % owners, col, step).start()
 
     @pl.when(jnp.logical_not(is_owner))
@@ -1408,7 +1408,7 @@
     channels = right.shape[1]
     hidden_width = w_expand.shape[1]
     block_rows = math.gcd(row_count, SUB)
-    bins_padded = -(-rel_table.shape[0] // 128) * 128
+    bins_padded = -(-rel_table.shape[0] // 16) * 16
     whole = lambda array: pl.BlockSpec(array.shape, lambda i: (0, 0))
     gain = pair_gain.reshape(1, channels)
     operands = (flags, rel, left, right, rel_table, gain, w_expand, w_contract)

time: 64.9 us -> 65.1 us (level)
  no operation moved by 1% of the time
where the time goes in v6:
time: 65.1 us; the launch traced here: 64.7 us
  Pallas kernels  64.7 us (99%)
    pallas_call x1, Pallas kernels, front_plane(): pl.pallas_call(functools.partial(plane_kernel, rows, cols, model_width),...  46.3 us
    pallas_call x1, Pallas kernels, banded_stage(): pl.pallas_call(banded_kernel, grid=(row_count // block_rows,), in_specs=[...  18.4 us

profile of v6, /device:TPU:0, one launch (start us, length us, event | category | flops | bytes accessed | tf_op | source)
XLA Modules:
  0.0 64.7 jit_solution(17887777151183685356)
XLA Ops:
  0.0 46.3 %shard_map.190 = (bf16[128,128]{1,0:T(8,128)(2,1)}, bf16[256,128]{1,0:T(8,128)(2,1)}, bf16[128,256,128]{2,1,0:T(8,128)(2,1)}, s32[8,128]{1,0:T(8,128)}) custom-call(bf16[128,2560]{1,0:T(8,128)(2,1)} %own_hbm.1, bf16[128,2560]{1,0:T(8,128)(2,1)} %own_hbm.1, f32[2560]{0:T(1024)} %attn_gain_ref.1, f32[128,128]{1,0:T(8,128)} %constant.8.clone.cos_ref, ...), custom_call_target="tpu_custom_call" | custom-call | tf_op jit(solution)/shard_map/pallas_call | solution.py:1479
  46.3 18.4 %shard_map.191 = bf16[128,256,128]{2,1,0:T(8,128)(2,1)} custom-call(s32[8,128]{1,0:T(8,128)} %get-tuple-element.9.flags, bf16[128,256,128]{2,1,0:T(8,128)(2,1)} %get-tuple-element.10.rel_ref, bf16[128,128]{1,0:T(8,128)(2,1)} %get-tuple-element.11.left_ref, bf16[256,128]{1,0:T(8,128)(2,1)} %get-tuple-element.12.right_ref, bf16[65,128]{1,0:T(8,128)(2,1)} %table_ref.3, ...), custom_call_target="tpu_custom_call" | custom-call | tf_op jit(solution)/shard_map/pallas_call | solution.py:1417
